TPU v7x, 32 devices: a whole 2x2x4 slice. The times are simulated.
32 devices in a mesh: dp: 2 (over core), blk: 4 (over y, x), head: 4 (over z).
Axes of the slice: x: 2, y: 2, z: 4, core: 2. Of those that a mesh axis runs over, the one named last changes fastest.
Arguments:
- activations: bfloat16 [2, 2, 2048, 1536], P(None, 'dp', ('blk', 'head')), may hold values from -6 to 6
- segments: int32 [2, 2, 2048], P(None, 'dp', 'blk'), may hold values from 0 to 15, never falling along the last dimension, each value on 1 to 1024 neighbouring positions
- cotangent: bfloat16 [2, 2, 2048, 1536], P(None, 'dp', ('blk', 'head')), may hold values from -6 to 6
- norm_gain_one: bfloat16 [1536], P(('dp', 'blk')), may hold values from 0.5 to 1.5
- query_weight: bfloat16 [1536, 1536], P(('dp', 'blk')), may hold values from -0.15625 to 0.15625
- key_weight: bfloat16 [1536, 768], P(('dp', 'blk')), may hold values from -0.15625 to 0.15625
- value_weight: bfloat16 [1536, 768], P(('dp', 'blk')), may hold values from -0.15625 to 0.15625
- output_weight: bfloat16 [1536, 1536], P(('dp', 'blk')), may hold values from -1.25 to 1.25
- norm_gain_two: bfloat16 [1536], P(('dp', 'blk')), may hold values from 0.5 to 1.5
- gate_weight: bfloat16 [1536, 4096], P(('dp', 'blk')), may hold values from -0.15625 to 0.15625
- up_weight: bfloat16 [1536, 4096], P(('dp', 'blk')), may hold values from -0.15625 to 0.15625
- down_weight: bfloat16 [4096, 1536], P(('dp', 'blk')), may hold values from -0.09375 to 0.09375
Outputs:
- block_out: bfloat16 [2, 2, 2048, 1536], P(None, 'dp', ('blk', 'head'))
- grad_input: bfloat16 [2, 2, 2048, 1536], P(None, 'dp', ('blk', 'head'))
- grad_gain_one: float32 [1536], P(('dp', 'blk'))
- grad_query: float32 [1536, 1536], P(('dp', 'blk'))
- grad_key: float32 [1536, 768], P(('dp', 'blk'))
- grad_value: float32 [1536, 768], P(('dp', 'blk'))
- grad_output: float32 [1536, 1536], P(('dp', 'blk'))
- grad_gain_two: float32 [1536], P(('dp', 'blk'))
- grad_gate: float32 [1536, 4096], P(('dp', 'blk'))
- grad_up: float32 [1536, 4096], P(('dp', 'blk'))
- grad_down: float32 [4096, 1536], P(('dp', 'blk'))
Inputs may be any that keep to these rules, and one draw needn't show every extreme that they name: `segments`: along each sequence the segment numbers never fall and every number is used; a document has at most 1024 tokens, and in every sequence one has exactly that many.
All inputs are finite; a program needn't handle non-finite values.
Results may differ from a plain program's by a relative error of at most 0.023.
Values may be sent and summed in bfloat16 or wider, within the bound.
No kernel may reach another device: no remote copies, remote signals or barrier semaphores. Data moves between devices by JAX's collectives and lax.ppermute only.
A program may use at most 320 MiB of HBM per device.

v0:
```python
import math
import jax
import jax.numpy as jnp
from jax import lax
from jax.sharding import PartitionSpec as P

D = 1536
QH = 16
KVH = 8
HD = 96
FF = 4096
EPS = 1e-05
NEG = -1e30


def shortened(value):
    return jax.tree.map(lambda a: a.astype(jnp.bfloat16) if a.dtype == jnp.float32 else a, value)


def plain_dot(left, right):
    return jnp.dot(left, right, preferred_element_type=jnp.float32)


def first_dot(left, right):
    return lax.dot_general(
        left, right, (((0,), (0,)), ((), ())), preferred_element_type=jnp.float32
    )


def last_dot(left, right):
    return lax.dot_general(
        left, right, (((1,), (1,)), ((), ())), preferred_element_type=jnp.float32
    )


def normalize(values):
    factor = lax.rsqrt(jnp.mean(values * values, -1, keepdims=True) + EPS)
    return (values * factor, factor)


def norm_back(grad_norm, gain, normed, factor):
    scaled = grad_norm * gain
    return factor * (scaled - normed * jnp.mean(scaled * normed, -1, keepdims=True))


def per_device(
    activations,
    segments,
    cotangent,
    norm_gain_one,
    query_weight,
    key_weight,
    value_weight,
    output_weight,
    norm_gain_two,
    gate_weight,
    up_weight,
    down_weight,
):
    shards = (
        norm_gain_one,
        query_weight,
        key_weight,
        value_weight,
        output_weight,
        norm_gain_two,
        gate_weight,
        up_weight,
        down_weight,
    )
    head_count = lax.axis_size("head")
    cycle_count = lax.axis_size("blk")
    tok_rows = activations.shape[2]
    span_len = tok_rows * head_count
    seq_len = span_len * cycle_count
    heads_here = QH // head_count
    kv_repeat = max(1, head_count // KVH)
    kv_here = KVH * kv_repeat // head_count
    group_size = heads_here // kv_here
    block_rows = span_len if span_len <= 1024 else 1024
    block_count = span_len // block_rows
    scale = 1.0 / math.sqrt(HD)
    first_pos = lax.axis_index("blk") * span_len
    full_shapes = (
        (D,),
        (D, QH * HD),
        (D, KVH * HD),
        (D, KVH * HD),
        (QH * HD, D),
        (D,),
        (D, FF),
        (D, FF),
        (FF, D),
    )
    totals = tuple((jnp.zeros(shape_full, jnp.float32) for shape_full in full_shapes))
    results = []
    grads_x = []
    for batch_index in range(activations.shape[0]):
        seg_rows = segments[batch_index, 0]
        cot_rows = cotangent[batch_index, 0]
        gain_one = lax.all_gather(shards[0], ("dp", "blk"), axis=0, tiled=True)
        query_w = lax.all_gather(shards[1], ("dp", "blk"), axis=0, tiled=True)
        key_w = lax.all_gather(shards[2], ("dp", "blk"), axis=0, tiled=True)
        value_w = lax.all_gather(shards[3], ("dp", "blk"), axis=0, tiled=True)
        out_w = lax.all_gather(shards[4], ("dp", "blk"), axis=0, tiled=True)
        gain_two = lax.all_gather(shards[5], ("dp", "blk"), axis=0, tiled=True)
        gate_w = lax.all_gather(shards[6], ("dp", "blk"), axis=0, tiled=True)
        up_w = lax.all_gather(shards[7], ("dp", "blk"), axis=0, tiled=True)
        down_w = lax.all_gather(shards[8], ("dp", "blk"), axis=0, tiled=True)
        gain_one_f = gain_one.astype(jnp.float32)
        gain_two_f = gain_two.astype(jnp.float32)
        x_float = activations[batch_index, 0].astype(jnp.float32)
        normed_one, factor_one = normalize(x_float)
        input_one = (normed_one * gain_one_f).astype(jnp.bfloat16)
        queries = plain_dot(input_one, query_w).astype(jnp.bfloat16).reshape(tok_rows, QH, HD)
        keys = plain_dot(input_one, key_w).astype(jnp.bfloat16).reshape(tok_rows, KVH, HD)
        values = plain_dot(input_one, value_w).astype(jnp.bfloat16).reshape(tok_rows, KVH, HD)
        if kv_repeat > 1:
            keys = jnp.repeat(keys, kv_repeat, axis=1)
            values = jnp.repeat(values, kv_repeat, axis=1)
        head_q = lax.all_to_all(queries, "head", split_axis=1, concat_axis=0, tiled=True)
        head_k = lax.all_to_all(keys, "head", split_axis=1, concat_axis=0, tiled=True)
        head_v = lax.all_to_all(values, "head", split_axis=1, concat_axis=0, tiled=True)
        query_blocks = head_q.reshape(block_count, block_rows, kv_here, group_size, HD)
        pos_blocks = (first_pos + jnp.arange(span_len, dtype=jnp.int32)).reshape(
            block_count, block_rows
        )
        seg_blocks = seg_rows.reshape(block_count, block_rows)
        key_piece = lax.all_gather(head_k, "blk", axis=0, tiled=True)
        value_piece = lax.all_gather(head_v, "blk", axis=0, tiled=True)
        seg_piece = lax.all_gather(seg_rows, "blk", axis=0, tiled=True)
        key_pos = jnp.arange(key_piece.shape[0], dtype=jnp.int32)

        def one_block(inputs):
            query_blk, query_pos, query_seg, run_max, run_sum, run_acc = inputs
            scores = (
                jnp.einsum(
                    "qhrd,khd->hrqk", query_blk, key_piece, preferred_element_type=jnp.float32
                )
                * scale
            )
            allowed = (key_pos[None, :] <= query_pos[:, None]) & (
                seg_piece[None, :] == query_seg[:, None]
            )
            new_max = jnp.maximum(run_max, jnp.max(jnp.where(allowed, scores, NEG), axis=-1))
            expo = jnp.where(allowed, jnp.exp(scores - new_max[..., None]), 0.0)
            decay = jnp.exp(run_max - new_max)
            new_sum = run_sum * decay + jnp.sum(expo, -1)
            new_acc = run_acc * decay[..., None] + jnp.einsum(
                "hrqk,khd->hrqd",
                expo.astype(jnp.bfloat16),
                value_piece,
                preferred_element_type=jnp.float32,
            )
            return (new_max, new_sum, new_acc)

        run_max, run_sum, run_acc = lax.map(
            one_block,
            (
                query_blocks,
                pos_blocks,
                seg_blocks,
                jnp.full((block_count, kv_here, group_size, block_rows), NEG, jnp.float32),
                jnp.zeros((block_count, kv_here, group_size, block_rows), jnp.float32),
                jnp.zeros((block_count, kv_here, group_size, block_rows, HD), jnp.float32),
            ),
        )
        attn_heads = run_acc / run_sum[..., None]
        log_total = run_max + jnp.log(run_sum)
        attn_low = (
            attn_heads.transpose(0, 3, 1, 2, 4)
            .reshape(span_len, heads_here, HD)
            .astype(jnp.bfloat16)
        )
        attn_tok = lax.all_to_all(
            attn_low, "head", split_axis=0, concat_axis=1, tiled=True
        ).reshape(tok_rows, QH * HD)
        x_mid = x_float + plain_dot(attn_tok, out_w)
        normed_two, factor_two = normalize(x_mid)
        input_two = (normed_two * gain_two_f).astype(jnp.bfloat16)
        gate_val = plain_dot(input_two, gate_w)
        up_val = plain_dot(input_two, up_w)
        sigma = jax.nn.sigmoid(gate_val)
        silu_val = gate_val * sigma
        hidden = (silu_val * up_val).astype(jnp.bfloat16)
        result = (x_mid + plain_dot(hidden, down_w)).astype(jnp.bfloat16)
        grad_down = first_dot(hidden, cot_rows)
        grad_hidden = last_dot(cot_rows, down_w)
        grad_gate_val = (grad_hidden * up_val * sigma * (1.0 + gate_val * (1.0 - sigma))).astype(
            jnp.bfloat16
        )
        grad_up_val = (grad_hidden * silu_val).astype(jnp.bfloat16)
        grad_gate_w = first_dot(input_two, grad_gate_val)
        grad_up_w = first_dot(input_two, grad_up_val)
        grad_input_two = last_dot(grad_gate_val, gate_w) + last_dot(grad_up_val, up_w)
        grad_gain_two = jnp.sum(grad_input_two * normed_two, 0)
        grad_mid = cot_rows.astype(jnp.float32) + norm_back(
            grad_input_two, gain_two_f, normed_two, factor_two
        )
        grad_branch = grad_mid.astype(jnp.bfloat16)
        grad_out_w = first_dot(attn_tok, grad_branch)
        grad_attn = last_dot(grad_branch, out_w).astype(jnp.bfloat16).reshape(tok_rows, QH, HD)
        grad_heads = lax.all_to_all(grad_attn, "head", split_axis=1, concat_axis=0, tiled=True)
        grad_blocks = grad_heads.reshape(block_count, block_rows, kv_here, group_size, HD)
        delta = jnp.sum(grad_blocks.astype(jnp.float32).transpose(0, 2, 3, 1, 4) * attn_heads, -1)
        full_k = lax.all_gather(head_k, "blk", axis=0, tiled=True)
        full_v = lax.all_gather(head_v, "blk", axis=0, tiled=True)
        full_seg = lax.all_gather(seg_rows, "blk", axis=0, tiled=True)
        key_k = full_k.reshape(cycle_count, span_len, kv_here, HD)
        key_v = full_v.reshape(cycle_count, span_len, kv_here, HD)
        key_seg = full_seg.reshape(cycle_count, span_len)
        key_pos = jnp.arange(seq_len, dtype=jnp.int32).reshape(cycle_count, span_len)

        def key_step(grad_total, key_inputs):
            blk_k, blk_v, blk_seg, blk_pos = key_inputs

            def query_step(carry, inputs):
                sum_k, sum_v = carry
                query_blk, query_pos, query_seg, lse_blk, delta_blk, grad_blk = inputs
                scores = (
                    jnp.einsum(
                        "qhrd,khd->hrqk", query_blk, blk_k, preferred_element_type=jnp.float32
                    )
                    * scale
                )
                allowed = (blk_pos[None, :] <= query_pos[:, None]) & (
                    blk_seg[None, :] == query_seg[:, None]
                )
                probs = jnp.where(allowed, jnp.exp(scores - lse_blk[..., None]), 0.0)
                grad_probs = jnp.einsum(
                    "qhrd,khd->hrqk", grad_blk, blk_v, preferred_element_type=jnp.float32
                )
                grad_scores = (probs * (grad_probs - delta_blk[..., None])).astype(jnp.bfloat16)
                grad_query = (
                    jnp.einsum(
                        "hrqk,khd->qhrd", grad_scores, blk_k, preferred_element_type=jnp.float32
                    )
                    * scale
                )
                sum_k = (
                    sum_k
                    + jnp.einsum(
                        "hrqk,qhrd->khd", grad_scores, query_blk, preferred_element_type=jnp.float32
                    )
                    * scale
                )
                sum_v = sum_v + jnp.einsum(
                    "hrqk,qhrd->khd",
                    probs.astype(jnp.bfloat16),
                    grad_blk,
                    preferred_element_type=jnp.float32,
                )
                return ((sum_k, sum_v), grad_query)

            empty_kv = jnp.zeros((span_len, kv_here, HD), jnp.float32)
            (sum_k, sum_v), grad_part = lax.scan(
                query_step,
                (empty_kv, empty_kv),
                (query_blocks, pos_blocks, seg_blocks, log_total, delta, grad_blocks),
            )
            return (grad_total + grad_part, (sum_k, sum_v))

        grad_start = jnp.zeros((block_count, block_rows, kv_here, group_size, HD), jnp.float32)
        grad_query, (sums_k, sums_v) = lax.scan(
            key_step, grad_start, (key_k, key_v, key_seg, key_pos)
        )
        sum_k = sums_k.reshape(seq_len, kv_here, HD)
        sum_v = sums_v.reshape(seq_len, kv_here, HD)
        owned_k = lax.psum_scatter(
            sum_k.astype(jnp.bfloat16), "blk", scatter_dimension=0, tiled=True
        ).astype(jnp.float32)
        owned_v = lax.psum_scatter(
            sum_v.astype(jnp.bfloat16), "blk", scatter_dimension=0, tiled=True
        ).astype(jnp.float32)
        grad_query = grad_query.reshape(span_len, heads_here, HD)
        tok_q = lax.all_to_all(
            grad_query.astype(jnp.bfloat16), "head", split_axis=0, concat_axis=1, tiled=True
        ).astype(grad_query.dtype)
        tok_k = lax.all_to_all(
            owned_k.astype(jnp.bfloat16), "head", split_axis=0, concat_axis=1, tiled=True
        ).astype(owned_k.dtype)
        tok_v = lax.all_to_all(
            owned_v.astype(jnp.bfloat16), "head", split_axis=0, concat_axis=1, tiled=True
        ).astype(owned_v.dtype)
        tok_q = tok_q.reshape(tok_rows, QH * HD).astype(jnp.bfloat16)
        tok_k = (
            jnp.sum(tok_k.reshape(tok_rows, KVH, kv_repeat, HD), 2)
            .reshape(tok_rows, KVH * HD)
            .astype(jnp.bfloat16)
        )
        tok_v = (
            jnp.sum(tok_v.reshape(tok_rows, KVH, kv_repeat, HD), 2)
            .reshape(tok_rows, KVH * HD)
            .astype(jnp.bfloat16)
        )
        grad_query_w = first_dot(input_one, tok_q)
        grad_key_w = first_dot(input_one, tok_k)
        grad_value_w = first_dot(input_one, tok_v)
        grad_input_one = (
            last_dot(tok_q, query_w) + last_dot(tok_k, key_w) + last_dot(tok_v, value_w)
        )
        grad_gain_one = jnp.sum(grad_input_one * normed_one, 0)
        grad_x = (grad_mid + norm_back(grad_input_one, gain_one_f, normed_one, factor_one)).astype(
            jnp.bfloat16
        )
        result, grad_x, terms = (
            result,
            grad_x,
            (
                grad_gain_one,
                grad_query_w,
                grad_key_w,
                grad_value_w,
                grad_out_w,
                grad_gain_two,
                grad_gate_w,
                grad_up_w,
                grad_down,
            ),
        )
        results.append(result)
        grads_x.append(grad_x)
        totals = tuple((left + right for left, right in zip(totals, terms)))
    owned = jax.tree.map(
        lambda part: part.astype(jnp.float32),
        lax.psum_scatter(shortened(totals), ("dp", "blk"), scatter_dimension=0, tiled=True),
    )
    owned = jax.tree.map(lambda part: part.astype(jnp.float32), lax.psum(shortened(owned), "head"))
    block_out = jnp.stack(results)[:, None]
    grad_input = jnp.stack(grads_x)[:, None]
    return (
        block_out,
        grad_input,
        owned[0],
        owned[1],
        owned[2],
        owned[3],
        owned[4],
        owned[5],
        owned[6],
        owned[7],
        owned[8],
    )


def solution(mesh):
    placed = (
        P(None, "dp", ("blk", "head"), None),
        P(None, "dp", "blk"),
        P(None, "dp", ("blk", "head"), None),
        P(("dp", "blk")),
        P(("dp", "blk"), None),
        P(("dp", "blk"), None),
        P(("dp", "blk"), None),
        P(("dp", "blk"), None),
        P(("dp", "blk")),
        P(("dp", "blk"), None),
        P(("dp", "blk"), None),
        P(("dp", "blk"), None),
    )
    return jax.shard_map(
        per_device,
        mesh=mesh,
        in_specs=placed,
        out_specs=(
            P(None, "dp", ("blk", "head"), None),
            P(None, "dp", ("blk", "head"), None),
            P(("dp", "blk")),
            P(("dp", "blk"), None),
            P(("dp", "blk"), None),
            P(("dp", "blk"), None),
            P(("dp", "blk"), None),
            P(("dp", "blk")),
            P(("dp", "blk"), None),
            P(("dp", "blk"), None),
            P(("dp", "blk"), None),
        ),
        check_vma=False,
    )
```

profile of v0, /device:TPU:0, one launch (start us, length us, event | category | flops | bytes accessed | tf_op | source)
XLA Modules:
  0.0 1429.7 jit_solution(12849763053035598999)
XLA Ops:
  13.7 16.3 %all-reduce.5 = (bf16[1536]{0:T(1024)(128)(2,1)S(1)}, bf16[1536]{0:T(1024)(128)(2,1)S(1)}) all-reduce(bf16[1536]{0:T(1024)(128)(2,1)S(1)} %dynamic-update-slice, bf16[1536]{0:T(1024)(128)(2,1)S(1)} %dynamic-update-slice.1), channel_id=1, replica_groups=mesh['dp'=2,'blk'=4,'head'=4] {'dp','blk'}, use_global_device_ids=true, to_apply=%add | all-reduce | flops 3072 | bytes 12288
  57.7 15.3 %all-gather.14.cloned.1.call-done = bf16[1536,768]{1,0:T(8,128)(2,1)} async-done(((bf16[192,768]{1,0:T(8,128)(2,1)}), bf16[1536,768]{1,0:T(8,128)(2,1)}) %all-gather.14.cloned.1.call-update) | async-done | bytes 2359312 | tf_op jit(solution)/shard_map/all_gather | solution.py:104
  105.3 13.9 all_gather.73
  119.2 14.7 %all_gather.74 = bf16[2048,2,96]{0,2,1:T(8,128)(2,1)} all-gather(bf16[512,2,96]{0,2,1:T(8,128)(2,1)S(1)} %all_to_all.220), channel_id=1, replica_groups=mesh['dp'=2,'blk'=4,'head'=4] {'blk'}, dimensions={0}, use_global_device_ids=true | all-gather | bytes 983040 | tf_op jit(solution)/shard_map/all_gather | solution.py:130
  144.3 20.2 %all_gather.63 = bf16[2048,2,96]{0,2,1:T(8,128)(2,1)} all-gather(bf16[512,2,96]{0,2,1:T(8,128)(2,1)S(1)} %all_to_all.199), channel_id=1, replica_groups=mesh['dp'=2,'blk'=4,'head'=4] {'blk'}, dimensions={0}, use_global_device_ids=true | all-gather | bytes 983040 | tf_op jit(solution)/shard_map/all_gather | solution.py:129
  164.8 11.4 all_gather.66
  258.6 55.3 %all-gather.20.cloned.1.call-done = bf16[1536,4096]{1,0:T(8,128)(2,1)} async-done(((bf16[192,4096]{1,0:T(8,128)(2,1)}), bf16[1536,4096]{1,0:T(8,128)(2,1)}) %all-gather.20.cloned.1.call-update) | async-done | bytes 12582928 | tf_op jit(solution)/shard_map/all_gather | solution.py:108
  321.6 66.3 %all-gather.22.cloned.1.call-done = bf16[4096,1536]{1,0:T(8,128)(2,1)} async-done(((bf16[512,1536]{1,0:T(8,128)(2,1)}), bf16[4096,1536]{1,0:T(8,128)(2,1)}) %all-gather.22.cloned.1.call-update) | async-done | bytes 12582928 | tf_op jit(solution)/shard_map/all_gather | solution.py:109
  387.9 11.4 multiply_convert_fusion.2
  399.4 10.5 fusion.214
  409.9 11.6 multiply_reduce_fusion.1
  432.2 9.9 multiply_convert_fusion
  489.3 50.1 %while.25 = (s32[]{:T(128)}, f32[1,512,2,2,96]{1,4,3,2,0:T(8,128)}, bf16[4,512,2,96]{1,3,2,0:T(8,128)(2,1)}, bf16[4,512,2,96]{1,3,2,0:T(8,128)(2,1)}, bf16[4,512...) while((s32[]{:T(128)}, f32[1,512,2,2,96]{1,4,3,2,0:T(8,128)}, ...), condition=%wide.region_18.19_spmd.clone, body=%wide.region_17.18_spmd.clone.sunk | while | flops 1018593792 | bytes 67217776 | solution.py:264
  545.2 46.2 %while.24 = (s32[]{:T(128)}, f32[1,512,2,2,96]{1,4,3,2,0:T(8,128)S(1)}, bf16[4,512,2,96]{1,3,2,0:T(8,128)(2,1)}, bf16[4,512,2,96]{1,3,2,0:T(8,128)(2,1)}, bf16[4...) while((s32[]{:T(128)}, ...), condition=%wide.region_11.12_spmd.clone, body=%wide.region_10.11_spmd.clone.sunk | while | flops 1018593792 | bytes 69314976 | solution.py:264
  604.0 16.3 %reduce-scatter.12.cloned.1.call-done = bf16[512,2,96]{0,2,1:T(8,128)(2,1)} async-done(((bf16[2048,2,96]{0,2,1:T(8,128)(2,1)}), bf16[512,2,96]{0,2,1:T(8,128)(2,1)}) %reduce-scatter.12.cloned.1.call-update) | async-done | bytes 196624 | tf_op jit(solution)/shard_map/reduce_scatter | solution.py:269
  639.1 10.6 reduce-scatter.18.cloned.1.call-done
  656.2 22.6 %reduce-scatter.14.cloned.1.call-done = bf16[512,2,96]{0,2,1:T(8,128)(2,1)} async-done(((bf16[2048,2,96]{0,2,1:T(8,128)(2,1)}), bf16[512,2,96]{0,2,1:T(8,128)(2,1)}) %reduce-scatter.14.cloned.1.call-update) | async-done | bytes 196624 | tf_op jit(solution)/shard_map/reduce_scatter | solution.py:272
  710.1 11.7 all-to-all-done.13
  725.7 12.8 all-to-all-done.9
  745.0 11.8 fusion.218
  756.8 14.7 %add_convert_fusion.2 = bf16[1536,4096]{1,0:T(8,128)(2,1)} fusion(f32[1536,4096]{1,0:T(8,128)} %fusion.218, bf16[128,1536]{1,0:T(8,128)(2,1)S(1)} %copy-done.16, bf16[128,4096]{1,0:T(8,128)(2,1)S(1)} %copy-done.37), kind=kOutput, calls=%fused_computation.80 | convolution fusion | flops 1623195648 | bytes 39190528 | tf_op jit(solution)/shard_map/dot_general | solution.py:25
  771.7 12.2 fusion.219
  783.9 16.2 %add_convert_fusion.1 = bf16[1536,4096]{1,0:T(8,128)(2,1)} fusion(f32[1536,4096]{1,0:T(8,128)} %fusion.219, bf16[128,1536]{1,0:T(8,128)(2,1)S(1)} %copy-done.16, bf16[128,4096]{1,0:T(8,128)(2,1)S(1)} %copy-done.35), kind=kOutput, calls=%fused_computation.79 | convolution fusion | flops 1623195648 | bytes 39190528 | tf_op jit(solution)/shard_map/dot_general | solution.py:25
  801.2 11.9 fusion.165
  813.2 15.4 %add_convert_fusion = bf16[4096,1536]{1,0:T(8,128)(2,1)} fusion(f32[4096,1536]{1,0:T(8,128)} %fusion.165, bf16[128,4096]{1,0:T(8,128)(2,1)S(1)} %copy-done.25, bf16[2,1,128,1536]{3,2,1,0:T(8,128)(2,1)S(1)} %copy-done.45), kind=kOutput, calls=%fused_computation.78 | convolution fusion | flops 1623195648 | bytes 39190528 | tf_op jit(solution)/shard_map/dot_general | solution.py:25
  829.1 57.6 %reduce-scatter.20.cloned.1.call-done = bf16[192,1536]{1,0:T(8,128)(2,1)} async-done(((bf16[1536,1536]{1,0:T(8,128)(2,1)}), bf16[192,1536]{1,0:T(8,128)(2,1)}) %reduce-scatter.20.cloned.1.call-update) | async-done | bytes 589840 | tf_op jit(solution)/shard_map/reduce_scatter | solution.py:326
  886.7 95.8 %reduce-scatter.28.cloned.1.call-done = bf16[192,4096]{1,0:T(8,128)(2,1)} async-done(((bf16[1536,4096]{1,0:T(8,128)(2,1)}), bf16[192,4096]{1,0:T(8,128)(2,1)}) %reduce-scatter.28.cloned.1.call-update) | async-done | bytes 1572880 | tf_op jit(solution)/shard_map/reduce_scatter | solution.py:326
  982.4 95.8 %reduce-scatter.30.cloned.1.call-done = bf16[192,4096]{1,0:T(8,128)(2,1)} async-done(((bf16[1536,4096]{1,0:T(8,128)(2,1)}), bf16[192,4096]{1,0:T(8,128)(2,1)}) %reduce-scatter.30.cloned.1.call-update) | async-done | bytes 1572880 | tf_op jit(solution)/shard_map/reduce_scatter | solution.py:326
  1078.2 95.8 %reduce-scatter.32.cloned.1.call-done = bf16[512,1536]{1,0:T(8,128)(2,1)} async-done(((bf16[4096,1536]{1,0:T(8,128)(2,1)}), bf16[512,1536]{1,0:T(8,128)(2,1)}) %reduce-scatter.32.cloned.1.call-update) | async-done | bytes 1572880 | tf_op jit(solution)/shard_map/reduce_scatter | solution.py:326
  1198.1 14.9 %all-reduce.4 = (bf16[1536]{0:T(1024)(128)(2,1)S(1)}, bf16[1536]{0:T(1024)(128)(2,1)S(1)}) all-reduce(bf16[1536]{0:T(1024)(128)(2,1)S(1)} %add_convert_fusion.6, bf16[1536]{0:T(1024)(128)(2,1)S(1)} %add_convert_fusion.5), channel_id=8, replica_groups=mesh['dp'=2,'blk'=4,'head'=4] {'dp','blk'}, use_global_device_ids=true, to_apply=%region_24.25.clone | all-reduce | flops 3072 | bytes 12288
  1213.2 12.1 all-reduce.6
  1229.1 179.4 %all-reduce.10.cloned.1.call-done = (bf16[192,1536]{1,0:T(8,128)(2,1)}, bf16[192,768]{1,0:T(8,128)(2,1)}, bf16[192,768]{1,0:T(8,128)(2,1)}, bf16[192,1536]{1,0:T...) async-done(((bf16[192,1536]{1,0:T(8,128)(2,1)}, bf16[192,768]{1,0:T(8,128)(2,1)}, bf16[192,768]{1,0:T(8,128)(2,1)}, ...) | async-done | bytes 6488080 | tf_op jit(solution)/shard_map/psum | solution.py:328
  (567 shorter events, 446.9 us)
Async XLA Ops:
  7.2 42.5 %all-gather.10.cloned.1.call-start = ((), (), s32[]{:S(2)}) async-start(), calls=%async_computation.27 | async-start | bytes 2654208 | tf_op jit(solution)/shard_map/all_gather | solution.py:103
  8.0 65.1 %all-gather.14.cloned.1.call-start = ((), (), s32[]{:S(2)}) async-start(), calls=%async_computation.29 | async-start | bytes 2654208 | tf_op jit(solution)/shard_map/all_gather | solution.py:104
  8.7 125.2 %all-gather.12.cloned.1.call-start = ((), (), s32[]{:S(2)}) async-start(), calls=%async_computation.28 | async-start | bytes 5308416 | tf_op jit(solution)/shard_map/all_gather | solution.py:102
  9.5 234.9 %all-gather.16.cloned.1.call-start = ((), (), s32[]{:S(2)}) async-start(), calls=%async_computation.30 | async-start | bytes 5308416 | tf_op jit(solution)/shard_map/all_gather | solution.py:105
  10.0 240.1 %all-gather.18.cloned.1.call-start = ((), (), s32[]{:S(2)}) async-start(), calls=%async_computation.31 | async-start | bytes 14155776 | tf_op jit(solution)/shard_map/all_gather | solution.py:107
  10.6 303.3 %all-gather.20.cloned.1.call-start = ((), (), s32[]{:S(2)}) async-start(), calls=%async_computation.32 | async-start | bytes 14155776 | tf_op jit(solution)/shard_map/all_gather | solution.py:108
  11.2 376.8 %all-gather.22.cloned.1.call-start = ((), (), s32[]{:S(2)}) async-start(), calls=%async_computation.33 | async-start | bytes 14155776 | tf_op jit(solution)/shard_map/all_gather | solution.py:109
  52.8 25.0 %all-to-all-start.4 = ((bf16[128,8,96]{0,2,1:T(8,128)(2,1)}), bf16[128,8,96]{0,2,1:T(8,128)(2,1)S(1)}, u32[]{:S(2)}, u32[]{:S(2)}) async-start(bf16[128,8,96]{0,2,1:T(8,128)(2,1)} %bitcast.29), calls=%async_computation.4 | async-start | bytes 393216 | tf_op jit(solution)/shard_map/all_to_all | solution.py:122
  100.8 37.3 %all-to-all-start.2 = ((bf16[128,8,96]{0,2,1:T(8,128)(2,1)}), bf16[128,8,96]{0,2,1:T(8,128)(2,1)S(1)}, u32[]{:S(2)}, u32[]{:S(2)}) async-start(bf16[128,8,96]{0,2,1:T(8,128)(2,1)} %bitcast.13), calls=%async_computation.2 | async-start | bytes 393216 | tf_op jit(solution)/shard_map/all_to_all | solution.py:123
  138.0 44.7 %all-to-all-start.5 = ((bf16[128,16,96]{0,2,1:T(8,128)(2,1)}), bf16[128,16,96]{0,2,1:T(8,128)(2,1)S(1)}, u32[]{:S(2)}, u32[]{:S(2)}) async-start(bf16[128,16,96]{0,2,1:T(8,128)(2,1)} %bitcast.34), calls=%async_computation.5 | async-start | bytes 786432 | tf_op jit(solution)/shard_map/all_to_all | solution.py:121
  182.7 22.0 %all-to-all-start.1 = ((bf16[128,16,96]{0,2,1:T(8,128)(2,1)}), bf16[128,16,96]{0,2,1:T(8,128)(2,1)}, u32[]{:S(2)}, u32[]{:S(2)}) async-start(bf16[128,16,96]{0,2,1:T(8,128)(2,1)} %bitcast.9), calls=%async_computation.1 | async-start | bytes 786432 | tf_op jit(solution)/shard_map/all_to_all | solution.py:121
  204.7 22.1 %all-to-all-start.7 = ((bf16[512,4,96]{2,1,0:T(4,128)(2,1)}), bf16[512,4,96]{2,1,0:T(4,128)(2,1)S(1)}, u32[]{:S(2)}, u32[]{:S(2)}) async-start(bf16[512,4,96]{2,1,0:T(4,128)(2,1)} %copy.196), calls=%async_computation.7 | async-start | bytes 1048576 | tf_op jit(solution)/shard_map/all_to_all | solution.py:175
  226.8 16.0 %all-to-all-start.3 = ((bf16[512,4,96]{2,1,0:T(4,128)(2,1)}), bf16[512,4,96]{2,1,0:T(4,128)(2,1)}, u32[]{:S(2)}, u32[]{:S(2)}) async-start(bf16[512,4,96]{2,1,0:T(4,128)(2,1)} %copy.186), calls=%async_computation.3 | async-start | bytes 1048576 | tf_op jit(solution)/shard_map/all_to_all | solution.py:175
  464.8 16.7 %all-to-all-start.12 = ((bf16[128,16,96]{0,2,1:T(8,128)(2,1)}), bf16[128,16,96]{0,2,1:T(8,128)(2,1)S(1)}, u32[]{:S(2)}, u32[]{:S(2)}) async-start(bf16[128,16,96]{0,2,1:T(8,128)(2,1)} %bitcast.78), calls=%async_computation.14 | async-start | bytes 786432 | tf_op jit(solution)/shard_map/all_to_all | solution.py:203
  481.5 60.2 %all-to-all-start.8 = ((bf16[128,16,96]{0,2,1:T(8,128)(2,1)}), bf16[128,16,96]{0,2,1:T(8,128)(2,1)}, u32[]{:S(2)}, u32[]{:S(2)}) async-start(bf16[128,16,96]{0,2,1:T(8,128)(2,1)} %bitcast.57), calls=%async_computation.8 | async-start | bytes 786432 | tf_op jit(solution)/shard_map/all_to_all | solution.py:203
  485.6 111.4 %reduce-scatter.16.cloned.1.call-start = ((), (), s32[]{:S(2)}) async-start(), calls=%async_computation.36 | async-start | bytes 983040 | tf_op jit(solution)/shard_map/reduce_scatter | solution.py:269
  541.7 78.7 %reduce-scatter.12.cloned.1.call-start = ((), (), s32[]{:S(2)}) async-start(), calls=%async_computation.34 | async-start | bytes 983040 | tf_op jit(solution)/shard_map/reduce_scatter | solution.py:269
  593.7 56.1 %reduce-scatter.18.cloned.1.call-start = ((), (), s32[]{:S(2)}) async-start(), calls=%async_computation.37 | async-start | bytes 983040 | tf_op jit(solution)/shard_map/reduce_scatter | solution.py:272
  596.0 82.8 %reduce-scatter.14.cloned.1.call-start = ((), (), s32[]{:S(2)}) async-start(), calls=%async_computation.35 | async-start | bytes 983040 | tf_op jit(solution)/shard_map/reduce_scatter | solution.py:272
  598.9 23.3 %all-to-all-start.14 = ((bf16[512,2,96]{2,1,0:T(2,128)(2,1)}), bf16[512,2,96]{2,1,0:T(2,128)(2,1)S(1)}, u32[]{:S(2)}, u32[]{:S(2)}) async-start(bf16[512,2,96]{2,1,0:T(2,128)(2,1)} %copy.222), calls=%async_computation.17 | async-start | bytes 524288 | tf_op jit(solution)/shard_map/all_to_all | solution.py:279
  622.2 13.5 all-to-all-start.10
  626.7 202.2 %reduce-scatter.22.cloned.1.call-start = ((), (), s32[]{:S(2)}) async-start(), calls=%async_computation.39 | async-start | bytes 2654208 | tf_op jit(solution)/shard_map/reduce_scatter | solution.py:326
  651.6 29.0 %all-to-all-start.15 = ((bf16[512,2,96]{2,1,0:T(2,128)(2,1)}), bf16[512,2,96]{2,1,0:T(2,128)(2,1)S(1)}, u32[]{:S(2)}, u32[]{:S(2)}) async-start(bf16[512,2,96]{2,1,0:T(2,128)(2,1)} %copy.226), calls=%async_computation.19 | async-start | bytes 524288 | tf_op jit(solution)/shard_map/all_to_all | solution.py:282
  685.2 143.8 %reduce-scatter.24.cloned.1.call-start = ((), (), s32[]{:S(2)}) async-start(), calls=%async_computation.40 | async-start | bytes 2654208 | tf_op jit(solution)/shard_map/reduce_scatter | solution.py:326
  697.6 131.5 %reduce-scatter.26.cloned.1.call-start = ((), (), s32[]{:S(2)}) async-start(), calls=%async_computation.41 | async-start | bytes 5308416 | tf_op jit(solution)/shard_map/reduce_scatter | solution.py:326
  705.5 16.4 %all-to-all-start.13 = ((bf16[512,4,96]{2,1,0:T(4,128)(2,1)}), bf16[512,4,96]{2,1,0:T(4,128)(2,1)S(1)}, u32[]{:S(2)}, u32[]{:S(2)}) async-start(bf16[512,4,96]{2,1,0:T(4,128)(2,1)} %bitcast.83), calls=%async_computation.15 | async-start | bytes 1048576 | tf_op jit(solution)/shard_map/all_to_all | solution.py:276
  721.9 16.6 %all-to-all-start.9 = ((bf16[512,4,96]{2,1,0:T(4,128)(2,1)}), bf16[512,4,96]{2,1,0:T(4,128)(2,1)S(1)}, u32[]{:S(2)}, u32[]{:S(2)}) async-start(bf16[512,4,96]{2,1,0:T(4,128)(2,1)} %bitcast.62), calls=%async_computation.9 | async-start | bytes 1048576 | tf_op jit(solution)/shard_map/all_to_all | solution.py:276
  725.4 161.3 %reduce-scatter.20.cloned.1.call-start = ((), (), s32[]{:S(2)}) async-start(), calls=%async_computation.38 | async-start | bytes 5308416 | tf_op jit(solution)/shard_map/reduce_scatter | solution.py:326
  744.0 238.4 %reduce-scatter.28.cloned.1.call-start = ((), (), s32[]{:S(2)}) async-start(), calls=%async_computation.42 | async-start | bytes 14155776 | tf_op jit(solution)/shard_map/reduce_scatter | solution.py:326
  771.5 306.7 %reduce-scatter.30.cloned.1.call-start = ((), (), s32[]{:S(2)}) async-start(), calls=%async_computation.43 | async-start | bytes 14155776 | tf_op jit(solution)/shard_map/reduce_scatter | solution.py:326
  800.1 373.9 %reduce-scatter.32.cloned.1.call-start = ((), (), s32[]{:S(2)}) async-start(), calls=%async_computation.44 | async-start | bytes 14155776 | tf_op jit(solution)/shard_map/reduce_scatter | solution.py:326
  828.7 579.8 %all-reduce.10.cloned.1.call-start = ((), (), s32[]{:S(2)}) async-start(), calls=%async_computation.45 | async-start | bytes 12976128 | tf_op jit(solution)/shard_map/psum | solution.py:328
  (139 other events, 2642.1 us)
Sparse Core Ops, SparseCore 0:
  9.9 32.1 all-gather.9
  44.0 28.9 all-gather.13
  75.0 42.0 all-gather.11
  118.8 46.9 all-gather.15
  167.5 72.4 all-gather.17
  241.7 72.1 all-gather.19
  315.8 72.1 all-gather.21
  541.8 26.5 reduce-scatter.15
  593.8 26.4 reduce-scatter.11
  623.7 26.0 reduce-scatter.17
  652.7 26.0 reduce-scatter.13
  682.6 42.4 reduce-scatter.21
  729.4 42.4 reduce-scatter.23
  775.2 53.8 reduce-scatter.25
  832.8 53.8 reduce-scatter.19
  890.0 92.3 reduce-scatter.27
  985.8 92.3 reduce-scatter.29
  1081.6 92.3 reduce-scatter.31
  1176.9 231.5 all-reduce.9
where the time goes:
time: 1440 us; the launch traced here: 1430 us
  waiting for transfers between devices  770 us (53%)
  matrix products  342 us (24%)
  blocking collectives  119 us (8%)
  starting transfers between devices  74.8 us (5%)
  local copies, waits for them, and re-layouts  70.3 us (5%)
  other arithmetic  35.4 us (2%)
  between operations  16.9 us (1%)
    reduce_scatter x7, waiting for transfers between devices, per_device(): lax.psum_scatter(shortened(totals), ('dp', 'blk'), scatter_dimension=0, t...  345 us
    psum x1, waiting for transfers between devices, per_device(): lax.psum(shortened(owned), 'head')  179 us
    dot_general x14, matrix products, first_dot(): lax.dot_general(left, right, (((0,), (0,)), ((), ())), preferred_element_...  98.8 us
    dot_general x14, matrix products, last_dot(): lax.dot_general(left, right, (((1,), (1,)), ((), ())), preferred_element_...  76.6 us
    all_gather x1, waiting for transfers between devices, per_device(): down_w = lax.all_gather(shards[8], ('dp', 'blk'), axis=0, tiled=True)  66.3 us
    dot_general x14, matrix products, plain_dot(): return jnp.dot(left, right, preferred_element_type=jnp.float32)  63.4 us
    all_gather x1, waiting for transfers between devices, per_device(): up_w = lax.all_gather(shards[7], ('dp', 'blk'), axis=0, tiled=True)  55.3 us
    all_gather x2, blocking collectives, per_device(): key_piece = lax.all_gather(head_k, 'blk', axis=0, tiled=True)  34.2 us
  transfers between devices with their start and end apart: 35, of which 19 were waited for; matrix products, arithmetic and copies ran while one was open for 24% of the time, Pallas kernels for 0%

commit v1 on v0

--- a/solution.py
+++ b/solution.py
@@ -11,6 +11,28 @@
 FF = 4096
 EPS = 1e-05
 NEG = -1e30
+
+
+def in_order(blocks, dim):
+    lengths = list(blocks.shape[1:])
+    lengths[dim] *= blocks.shape[0]
+    return jnp.moveaxis(blocks, 0, dim).reshape(lengths)
+
+
+def gather_around(x, axis, dim):
+    size = lax.axis_size(axis)
+    pairs = [(i, (i + 1) % size) for i in range(size)]
+    back = [(b, a) for a, b in pairs]
+    lower, upper = ([], [])
+    for hop in range(size - 1):
+        if hop % 2 == 0:
+            lower.append(lax.ppermute(lower[-1] if lower else x, axis, pairs))
+        else:
+            upper.append(lax.ppermute(upper[-1] if upper else x, axis, back))
+    blocks = jnp.stack([*lower[::-1], x, *upper])
+    shift = lax.axis_index(axis) - len(lower)
+    blocks = blocks[(jnp.arange(size) - shift) % size]
+    return in_order(blocks, dim)
 
 
 def shortened(value):
@@ -106,7 +128,7 @@
         gain_two = lax.all_gather(shards[5], ("dp", "blk"), axis=0, tiled=True)
         gate_w = lax.all_gather(shards[6], ("dp", "blk"), axis=0, tiled=True)
         up_w = lax.all_gather(shards[7], ("dp", "blk"), axis=0, tiled=True)
-        down_w = lax.all_gather(shards[8], ("dp", "blk"), axis=0, tiled=True)
+        down_w = gather_around(shards[8], ("dp", "blk"), 0)
         gain_one_f = gain_one.astype(jnp.float32)
         gain_two_f = gain_two.astype(jnp.float32)
         x_float = activations[batch_index, 0].astype(jnp.float32)

time: 1440 us -> 1630 us (1.13)
  blocking collectives: 119 us -> 321 us
  waiting for transfers between devices: 770 us -> 726 us
  local copies, waits for them, and re-layouts: 70.3 us -> 110 us
  matrix products: 342 us -> 324 us
    all_gather x2, blocking collectives: 15.8 us -> 111 us  [per_device(): seg_piece = lax.all_gather(seg_rows, 'blk', axis=0, tiled=True)]
    ppermute x0 -> x7, waiting for transfers between devices: none -> 90.2 us  [the longest x4 90.2 us: gather_around(): lower.append(lax.ppermute(lower[-1] if lower else x, axis, pairs))]
    all_gather x1 -> x0, waiting for transfers between devices: 66.3 us -> none  [per_device(): down_w = lax.all_gather(shards[8], ('dp', 'blk'), axis=0, tiled=True)]
    all_gather x2, blocking collectives: 34.2 us -> 99.5 us  [per_device(): key_piece = lax.all_gather(head_k, 'blk', axis=0, tiled=True)]
    all_gather x1, waiting for transfers between devices: 55.3 us -> 0.01 us  [per_device(): up_w = lax.all_gather(shards[7], ('dp', 'blk'), axis=0, tiled=True)]
    unnamed x2, blocking collectives: 31.2 us -> 70.2 us
    unnamed x167 -> x184, local copies, waits for them, and re-layouts: 5.38 us -> 25.2 us
  transfers between devices with their start and end apart: 35 -> 41, of which waited for: 19 -> 21; matrix products, arithmetic and copies ran while one was open for 24% -> 22% of each run, Pallas kernels for 0% -> 0%
where the time goes in v1:
time: 1630 us; the launch traced here: 1620 us
  waiting for transfers between devices  726 us (45%)
  matrix products  324 us (20%)
  blocking collectives  321 us (20%)
  local copies, waits for them, and re-layouts  110 us (7%)
  starting transfers between devices  82.5 us (5%)
  other arithmetic  39.5 us (2%)
  between operations  17.5 us (1%)
    reduce_scatter x7, waiting for transfers between devices, per_device(): lax.psum_scatter(shortened(totals), ('dp', 'blk'), scatter_dimension=0, t...  345 us
    psum x1, waiting for transfers between devices, per_device(): lax.psum(shortened(owned), 'head')  179 us
    all_gather x2, blocking collectives, per_device(): seg_piece = lax.all_gather(seg_rows, 'blk', axis=0, tiled=True)  111 us
    all_gather x2, blocking collectives, per_device(): key_piece = lax.all_gather(head_k, 'blk', axis=0, tiled=True)  99.5 us
    dot_general x14, matrix products, first_dot(): lax.dot_general(left, right, (((0,), (0,)), ((), ())), preferred_element_...  98.8 us
    ppermute x4, waiting for transfers between devices, gather_around(): lower.append(lax.ppermute(lower[-1] if lower else x, axis, pairs))  90.2 us
    unnamed x2, blocking collectives  70.2 us
    dot_general x14, matrix products, last_dot(): lax.dot_general(left, right, (((1,), (1,)), ((), ())), preferred_element_...  64.2 us
  transfers between devices with their start and end apart: 41, of which 21 were waited for; matrix products, arithmetic and copies ran while one was open for 22% of the time, Pallas kernels for 0%

profile of v1, /device:TPU:0, one launch (start us, length us, event | category | flops | bytes accessed | tf_op | source)
XLA Modules:
  0.0 1621.0 jit_solution(9110955388017164264)
XLA Ops:
  13.7 44.3 %collective-permute-done = bf16[512,1536]{1,0:T(8,128)(2,1)} collective-permute-done((bf16[512,1536]{1,0:T(8,128)(2,1)}, bf16[512,1536]{1,0:T(8,128)(2,1)}, u32[]{:S(2)}, u32[]{:S(2)}) %collective-permute-start) | collective-permute-done | bytes 1572896 | tf_op jit(solution)/shard_map/ppermute | solution.py:29
  60.6 45.9 %collective-permute-done.1 = bf16[512,1536]{1,0:T(8,128)(2,1)} collective-permute-done((bf16[512,1536]{1,0:T(8,128)(2,1)}, bf16[512,1536]{1,0:T(8,128)(2,1)}, u32[]{:S(2)}, u32[]{:S(2)}) %collective-permute-start.1) | collective-permute-done | bytes 1572896 | tf_op jit(solution)/shard_map/ppermute | solution.py:29
  109.6 103.3 %all-gather = s32[1,1,2048]{2,1,0:T(1,128)S(1)} all-gather(s32[1,1,512]{2,1,0:T(1,128)S(1)} %get-tuple-element.709), channel_id=2, replica_groups=mesh['dp'=2,'blk'=4,'head'=4] {'blk'}, dimensions={2}, use_global_device_ids=true | all-gather | bytes 10240 | tf_op jit(solution)/shard_map/all_gather | solution.py:153
  227.5 55.2 %all-reduce.5 = (bf16[1536]{0:T(1024)(128)(2,1)S(1)}, bf16[1536]{0:T(1024)(128)(2,1)S(1)}) all-reduce(bf16[1536]{0:T(1024)(128)(2,1)S(1)} %dynamic-update-slice, bf16[1536]{0:T(1024)(128)(2,1)S(1)} %dynamic-update-slice.1), channel_id=1, replica_groups=mesh['dp'=2,'blk'=4,'head'=4] {'dp','blk'}, use_global_device_ids=true, to_apply=%add | all-reduce | flops 3072 | bytes 12288
  330.6 80.6 %all_gather.68 = bf16[2048,2,96]{0,2,1:T(8,128)(2,1)S(1)} all-gather(bf16[512,2,96]{0,2,1:T(8,128)(2,1)S(1)} %all_to_all.213), channel_id=1, replica_groups=mesh['dp'=2,'blk'=4,'head'=4] {'blk'}, dimensions={0}, use_global_device_ids=true | all-gather | bytes 983040 | tf_op jit(solution)/shard_map/all_gather | solution.py:151
  412.1 17.3 %all_gather.69 = bf16[2048,2,96]{0,2,1:T(8,128)(2,1)S(1)} all-gather(bf16[512,2,96]{0,2,1:T(8,128)(2,1)S(1)} %all_to_all.220), channel_id=1, replica_groups=mesh['dp'=2,'blk'=4,'head'=4] {'blk'}, dimensions={0}, use_global_device_ids=true | all-gather | bytes 983040 | tf_op jit(solution)/shard_map/all_gather | solution.py:152
  431.3 18.9 %all_gather.59 = bf16[2048,2,96]{0,2,1:T(8,128)(2,1)S(1)} all-gather(bf16[512,2,96]{0,2,1:T(8,128)(2,1)S(1)} %all_to_all.199), channel_id=1, replica_groups=mesh['dp'=2,'blk'=4,'head'=4] {'blk'}, dimensions={0}, use_global_device_ids=true | all-gather | bytes 983040 | tf_op jit(solution)/shard_map/all_gather | solution.py:151
  452.1 10.7 all_gather.62
  548.8 11.4 gather_fusion
  582.2 10.5 multiply_convert_fusion.2
  597.9 11.6 multiply_reduce_fusion.1
  633.5 10.4 multiply_reduce_fusion
  668.7 54.9 %while.25 = (s32[]{:T(128)}, f32[1,512,2,2,96]{1,4,3,2,0:T(8,128)}, bf16[4,512,2,96]{1,3,2,0:T(8,128)(2,1)}, bf16[4,512,2,96]{1,3,2,0:T(8,128)(2,1)}, bf16[4,512...) while((s32[]{:T(128)}, f32[1,512,2,2,96]{1,4,3,2,0:T(8,128)}, ...), condition=%wide.region_18.19_spmd.clone, body=%wide.region_17.18_spmd.clone.sunk | while | flops 1018593792 | bytes 67217776 | solution.py:286
  730.5 51.0 %while.24 = (s32[]{:T(128)}, f32[1,512,2,2,96]{1,4,3,2,0:T(8,128)S(1)}, bf16[4,512,2,96]{1,3,2,0:T(8,128)(2,1)}, bf16[4,512,2,96]{1,3,2,0:T(8,128)(2,1)}, bf16[4...) while((s32[]{:T(128)}, ...), condition=%wide.region_11.12_spmd.clone, body=%wide.region_10.11_spmd.clone.sunk | while | flops 1018593792 | bytes 69314976 | solution.py:286
  793.9 16.7 %reduce-scatter.12.cloned.1.call-done = bf16[512,2,96]{0,2,1:T(8,128)(2,1)} async-done(((bf16[2048,2,96]{0,2,1:T(8,128)(2,1)}), bf16[512,2,96]{0,2,1:T(8,128)(2,1)}) %reduce-scatter.12.cloned.1.call-update) | async-done | bytes 196624 | tf_op jit(solution)/shard_map/reduce_scatter | solution.py:291
  829.4 10.8 reduce-scatter.18.cloned.1.call-done
  846.6 23.0 %reduce-scatter.14.cloned.1.call-done = bf16[512,2,96]{0,2,1:T(8,128)(2,1)} async-done(((bf16[2048,2,96]{0,2,1:T(8,128)(2,1)}), bf16[512,2,96]{0,2,1:T(8,128)(2,1)}) %reduce-scatter.14.cloned.1.call-update) | async-done | bytes 196624 | tf_op jit(solution)/shard_map/reduce_scatter | solution.py:294
  900.6 11.9 all-to-all-done.13
  916.3 12.9 all-to-all-done.9
  935.8 11.8 fusion.218
  947.6 14.7 add_convert_fusion.2
  962.6 12.1 fusion.219
  974.7 16.3 %add_convert_fusion.1 = bf16[1536,4096]{1,0:T(8,128)(2,1)} fusion(f32[1536,4096]{1,0:T(8,128)} %fusion.219, bf16[128,1536]{1,0:T(8,128)(2,1)S(1)} %copy-done.16, bf16[128,4096]{1,0:T(8,128)(2,1)S(1)} %copy-done.34), kind=kOutput, calls=%fused_computation.80 | convolution fusion | flops 1623195648 | bytes 39190528 | tf_op jit(solution)/shard_map/dot_general | solution.py:47
  992.1 11.9 fusion.164
  1004.1 15.5 add_convert_fusion
  1020.1 57.6 %reduce-scatter.20.cloned.1.call-done = bf16[192,1536]{1,0:T(8,128)(2,1)} async-done(((bf16[1536,1536]{1,0:T(8,128)(2,1)}), bf16[192,1536]{1,0:T(8,128)(2,1)}) %reduce-scatter.20.cloned.1.call-update) | async-done | bytes 589840 | tf_op jit(solution)/shard_map/reduce_scatter | solution.py:348
  1077.7 95.8 %reduce-scatter.28.cloned.1.call-done = bf16[192,4096]{1,0:T(8,128)(2,1)} async-done(((bf16[1536,4096]{1,0:T(8,128)(2,1)}), bf16[192,4096]{1,0:T(8,128)(2,1)}) %reduce-scatter.28.cloned.1.call-update) | async-done | bytes 1572880 | tf_op jit(solution)/shard_map/reduce_scatter | solution.py:348
  1173.5 95.8 %reduce-scatter.30.cloned.1.call-done = bf16[192,4096]{1,0:T(8,128)(2,1)} async-done(((bf16[1536,4096]{1,0:T(8,128)(2,1)}), bf16[192,4096]{1,0:T(8,128)(2,1)}) %reduce-scatter.30.cloned.1.call-update) | async-done | bytes 1572880 | tf_op jit(solution)/shard_map/reduce_scatter | solution.py:348
  1269.2 95.8 %reduce-scatter.32.cloned.1.call-done = bf16[512,1536]{1,0:T(8,128)(2,1)} async-done(((bf16[4096,1536]{1,0:T(8,128)(2,1)}), bf16[512,1536]{1,0:T(8,128)(2,1)}) %reduce-scatter.32.cloned.1.call-update) | async-done | bytes 1572880 | tf_op jit(solution)/shard_map/reduce_scatter | solution.py:348
  1389.1 14.9 all-reduce.4
  1404.2 12.2 all-reduce.6
  1420.1 179.3 %all-reduce.10.cloned.1.call-done = (bf16[192,1536]{1,0:T(8,128)(2,1)}, bf16[192,768]{1,0:T(8,128)(2,1)}, bf16[192,768]{1,0:T(8,128)(2,1)}, bf16[192,1536]{1,0:T...) async-done(((bf16[192,1536]{1,0:T(8,128)(2,1)}, bf16[192,768]{1,0:T(8,128)(2,1)}, bf16[192,768]{1,0:T(8,128)(2,1)}, ...) | async-done | bytes 6488080 | tf_op jit(solution)/shard_map/psum | solution.py:350
  (600 shorter events, 473.1 us)
Async XLA Ops:
  7.2 276.2 %all-gather.9.cloned.1.call-start = ((), (), s32[]{:S(2)}) async-start(), calls=%async_computation.27 | async-start | bytes 2654208 | tf_op jit(solution)/shard_map/all_gather | solution.py:125
  8.0 285.4 %all-gather.13.cloned.1.call-start = ((), (), s32[]{:S(2)}) async-start(), calls=%async_computation.29 | async-start | bytes 2654208 | tf_op jit(solution)/shard_map/all_gather | solution.py:126
  8.7 470.7 %all-gather.11.cloned.1.call-start = ((), (), s32[]{:S(2)}) async-start(), calls=%async_computation.28 | async-start | bytes 5308416 | tf_op jit(solution)/shard_map/all_gather | solution.py:124
  9.5 552.5 %all-gather.15.cloned.1.call-start = ((), (), s32[]{:S(2)}) async-start(), calls=%async_computation.30 | async-start | bytes 5308416 | tf_op jit(solution)/shard_map/all_gather | solution.py:127
  10.0 557.7 %all-gather.17.cloned.1.call-start = ((), (), s32[]{:S(2)}) async-start(), calls=%async_computation.31 | async-start | bytes 14155776 | tf_op jit(solution)/shard_map/all_gather | solution.py:129
  10.6 564.9 %all-gather.19.cloned.1.call-start = ((), (), s32[]{:S(2)}) async-start(), calls=%async_computation.32 | async-start | bytes 14155776 | tf_op jit(solution)/shard_map/all_gather | solution.py:130
  10.7 47.3 %collective-permute-start = (bf16[512,1536]{1,0:T(8,128)(2,1)}, bf16[512,1536]{1,0:T(8,128)(2,1)}, u32[]{:S(2)}, u32[]{:S(2)}) collective-permute-start(bf16[512,1536]{1,0:T(8,128)(2,1)} %param.27), channel_id=1, source_target_pairs={{0,4},{4,8},{8,12},{12,16},{16,20},{20,24},{24,28},{28,0},{1,5},{5... | collective-permute-start | bytes 4718600 | tf_op jit(solution)/shard_map/ppermute | solution.py:29
  58.0 48.6 %collective-permute-start.1 = (bf16[512,1536]{1,0:T(8,128)(2,1)}, bf16[512,1536]{1,0:T(8,128)(2,1)}, u32[]{:S(2)}, u32[]{:S(2)}) collective-permute-start(bf16[512,1536]{1,0:T(8,128)(2,1)} %collective-permute-done), channel_id=1, source_target_pairs={{0,4},{4,8},{8,12},{12,16},{16,20},{20,24},{24,28},{28,0},{1,5},{5... | collective-permute-start | bytes 4718600 | tf_op jit(solution)/shard_map/ppermute | solution.py:29
  59.6 164.2 %collective-permute-start.4 = (bf16[512,1536]{1,0:T(8,128)(2,1)S(1)}, bf16[512,1536]{1,0:T(8,128)(2,1)}, u32[]{:S(2)}, u32[]{:S(2)}) collective-permute-start(bf16[512,1536]{1,0:T(8,128)(2,1)S(1)} %copy-done.66), channel_id=1, source_target_pairs={{4,0},{8,4},{12,8},{16,12},{20,16},{24,20},{28,24},{0,28},{5,1},{9... | collective-permute-start | bytes 4718600 | tf_op jit(solution)/shard_map/ppermute | solution.py:31
  106.5 185.5 %collective-permute-start.2 = (bf16[512,1536]{1,0:T(8,128)(2,1)}, bf16[512,1536]{1,0:T(8,128)(2,1)}, u32[]{:S(2)}, u32[]{:S(2)}) collective-permute-start(bf16[512,1536]{1,0:T(8,128)(2,1)} %collective-permute-done.1), channel_id=1, source_target_pairs={{0,4},{4,8},{8,12},{12,16},{16,20},{20,24},{24,28},{28,0},{1,5},{5... | collective-permute-start | bytes 4718600 | tf_op jit(solution)/shard_map/ppermute | solution.py:29
  223.8 100.4 %collective-permute-start.5 = (bf16[512,1536]{1,0:T(8,128)(2,1)}, bf16[512,1536]{1,0:T(8,128)(2,1)}, u32[]{:S(2)}, u32[]{:S(2)}) collective-permute-start(bf16[512,1536]{1,0:T(8,128)(2,1)} %collective-permute-done.4), channel_id=1, source_target_pairs={{4,0},{8,4},{12,8},{16,12},{20,16},{24,20},{28,24},{0,28},{5,1},{9... | collective-permute-start | bytes 4718600 | tf_op jit(solution)/shard_map/ppermute | solution.py:31
  292.0 172.6 %collective-permute-start.3 = (bf16[512,1536]{1,0:T(8,128)(2,1)}, bf16[512,1536]{1,0:T(8,128)(2,1)}, u32[]{:S(2)}, u32[]{:S(2)}) collective-permute-start(bf16[512,1536]{1,0:T(8,128)(2,1)} %collective-permute-done.2), channel_id=1, source_target_pairs={{0,4},{4,8},{8,12},{12,16},{16,20},{20,24},{24,28},{28,0},{1,5},{5... | collective-permute-start | bytes 4718600 | tf_op jit(solution)/shard_map/ppermute | solution.py:29
  324.2 222.0 %collective-permute-start.6 = (bf16[512,1536]{1,0:T(8,128)(2,1)}, bf16[512,1536]{1,0:T(8,128)(2,1)}, u32[]{:S(2)}, u32[]{:S(2)}) collective-permute-start(bf16[512,1536]{1,0:T(8,128)(2,1)} %collective-permute-done.5), channel_id=1, source_target_pairs={{4,0},{8,4},{12,8},{16,12},{20,16},{24,20},{28,24},{0,28},{5,1},{9... | collective-permute-start | bytes 4718600 | tf_op jit(solution)/shard_map/ppermute | solution.py:31
  497.6 21.4 %all-to-all-start.1 = ((bf16[128,16,96]{0,2,1:T(8,128)(2,1)}), bf16[128,16,96]{0,2,1:T(8,128)(2,1)}, u32[]{:S(2)}, u32[]{:S(2)}) async-start(bf16[128,16,96]{0,2,1:T(8,128)(2,1)} %bitcast.9), calls=%async_computation.1 | async-start | bytes 786432 | tf_op jit(solution)/shard_map/all_to_all | solution.py:143
  519.0 22.1 %all-to-all-start.7 = ((bf16[512,4,96]{2,1,0:T(4,128)(2,1)}), bf16[512,4,96]{2,1,0:T(4,128)(2,1)S(1)}, u32[]{:S(2)}, u32[]{:S(2)}) async-start(bf16[512,4,96]{2,1,0:T(4,128)(2,1)} %copy.204), calls=%async_computation.7 | async-start | bytes 1048576 | tf_op jit(solution)/shard_map/all_to_all | solution.py:197
  541.1 20.5 %all-to-all-start.3 = ((bf16[512,4,96]{2,1,0:T(4,128)(2,1)}), bf16[512,4,96]{2,1,0:T(4,128)(2,1)S(1)}, u32[]{:S(2)}, u32[]{:S(2)}) async-start(bf16[512,4,96]{2,1,0:T(4,128)(2,1)} %copy.194), calls=%async_computation.3 | async-start | bytes 1048576 | tf_op jit(solution)/shard_map/all_to_all | solution.py:197
  660.9 65.0 %all-to-all-start.8 = ((bf16[128,16,96]{0,2,1:T(8,128)(2,1)}), bf16[128,16,96]{0,2,1:T(8,128)(2,1)}, u32[]{:S(2)}, u32[]{:S(2)}) async-start(bf16[128,16,96]{0,2,1:T(8,128)(2,1)} %bitcast.68), calls=%async_computation.8 | async-start | bytes 786432 | tf_op jit(solution)/shard_map/all_to_all | solution.py:225
  665.0 122.0 %reduce-scatter.16.cloned.1.call-start = ((), (), s32[]{:S(2)}) async-start(), calls=%async_computation.35 | async-start | bytes 983040 | tf_op jit(solution)/shard_map/reduce_scatter | solution.py:291
  725.8 84.8 %reduce-scatter.12.cloned.1.call-start = ((), (), s32[]{:S(2)}) async-start(), calls=%async_computation.33 | async-start | bytes 983040 | tf_op jit(solution)/shard_map/reduce_scatter | solution.py:291
  783.8 56.4 %reduce-scatter.18.cloned.1.call-start = ((), (), s32[]{:S(2)}) async-start(), calls=%async_computation.36 | async-start | bytes 983040 | tf_op jit(solution)/shard_map/reduce_scatter | solution.py:294
  786.0 83.6 %reduce-scatter.14.cloned.1.call-start = ((), (), s32[]{:S(2)}) async-start(), calls=%async_computation.34 | async-start | bytes 983040 | tf_op jit(solution)/shard_map/reduce_scatter | solution.py:294
  788.9 23.5 %all-to-all-start.14 = ((bf16[512,2,96]{2,1,0:T(2,128)(2,1)}), bf16[512,2,96]{2,1,0:T(2,128)(2,1)S(1)}, u32[]{:S(2)}, u32[]{:S(2)}) async-start(bf16[512,2,96]{2,1,0:T(2,128)(2,1)} %copy.232), calls=%async_computation.17 | async-start | bytes 524288 | tf_op jit(solution)/shard_map/all_to_all | solution.py:301
  817.0 202.9 %reduce-scatter.22.cloned.1.call-start = ((), (), s32[]{:S(2)}) async-start(), calls=%async_computation.38 | async-start | bytes 2654208 | tf_op jit(solution)/shard_map/reduce_scatter | solution.py:348
  842.0 29.4 %all-to-all-start.15 = ((bf16[512,2,96]{2,1,0:T(2,128)(2,1)}), bf16[512,2,96]{2,1,0:T(2,128)(2,1)S(1)}, u32[]{:S(2)}, u32[]{:S(2)}) async-start(bf16[512,2,96]{2,1,0:T(2,128)(2,1)} %copy.236), calls=%async_computation.19 | async-start | bytes 524288 | tf_op jit(solution)/shard_map/all_to_all | solution.py:304
  876.0 143.9 %reduce-scatter.24.cloned.1.call-start = ((), (), s32[]{:S(2)}) async-start(), calls=%async_computation.39 | async-start | bytes 2654208 | tf_op jit(solution)/shard_map/reduce_scatter | solution.py:348
  888.4 131.6 %reduce-scatter.26.cloned.1.call-start = ((), (), s32[]{:S(2)}) async-start(), calls=%async_computation.40 | async-start | bytes 5308416 | tf_op jit(solution)/shard_map/reduce_scatter | solution.py:348
  912.5 16.8 %all-to-all-start.9 = ((bf16[512,4,96]{2,1,0:T(4,128)(2,1)}), bf16[512,4,96]{2,1,0:T(4,128)(2,1)S(1)}, u32[]{:S(2)}, u32[]{:S(2)}) async-start(bf16[512,4,96]{2,1,0:T(4,128)(2,1)} %bitcast.73), calls=%async_computation.9 | async-start | bytes 1048576 | tf_op jit(solution)/shard_map/all_to_all | solution.py:298
  916.0 161.7 %reduce-scatter.20.cloned.1.call-start = ((), (), s32[]{:S(2)}) async-start(), calls=%async_computation.37 | async-start | bytes 5308416 | tf_op jit(solution)/shard_map/reduce_scatter | solution.py:348
  934.8 238.6 %reduce-scatter.28.cloned.1.call-start = ((), (), s32[]{:S(2)}) async-start(), calls=%async_computation.41 | async-start | bytes 14155776 | tf_op jit(solution)/shard_map/reduce_scatter | solution.py:348
  962.4 306.9 %reduce-scatter.30.cloned.1.call-start = ((), (), s32[]{:S(2)}) async-start(), calls=%async_computation.42 | async-start | bytes 14155776 | tf_op jit(solution)/shard_map/reduce_scatter | solution.py:348
  991.0 374.0 %reduce-scatter.32.cloned.1.call-start = ((), (), s32[]{:S(2)}) async-start(), calls=%async_computation.43 | async-start | bytes 14155776 | tf_op jit(solution)/shard_map/reduce_scatter | solution.py:348
  1019.6 579.8 %all-reduce.10.cloned.1.call-start = ((), (), s32[]{:S(2)}) async-start(), calls=%async_computation.44 | async-start | bytes 12976128 | tf_op jit(solution)/shard_map/psum | solution.py:350
  (150 other events, 3789.0 us)
Sparse Core Ops, SparseCore 0:
  10.0 42.2 all-gather.8
  54.1 38.4 all-gather.12
  94.5 56.7 all-gather.10
  153.1 58.6 all-gather.14
  213.5 140.7 all-gather.16
  356.1 103.1 all-gather.18
  726.0 26.6 reduce-scatter.15
  783.9 26.6 reduce-scatter.11
  814.1 26.0 reduce-scatter.17
  843.5 26.0 reduce-scatter.13
  873.6 42.4 reduce-scatter.21
  920.2 42.4 reduce-scatter.23
  966.2 53.8 reduce-scatter.25
  1023.8 53.8 reduce-scatter.19
  1081.0 92.4 reduce-scatter.27
  1176.8 92.3 reduce-scatter.29
  1272.6 92.3 reduce-scatter.31
  1367.8 231.5 all-reduce.9
